TPU v7x, 32 devices: a whole 2x2x4 slice. The times are simulated.
32 devices in a mesh: rep: 4 (over y, core), ep: 8 (over z, x).
Axes of the slice: x: 2, y: 2, z: 4, core: 2. Of those that a mesh axis runs over, the one named last changes fastest.
Arguments:
- tokens: bfloat16 [4096, 1024], P(('rep', 'ep')), may hold values from -6 to 6
- expert_ids: int32 [4096, 8], P(('rep', 'ep')), may hold values from 0 to 15, all different within a row; in each aligned block of 128 rows (0 to 127, 128 to 255, ...) at most 96 rows name the same one
- route_weights: float32 [4096, 8], P(('rep', 'ep')), may hold values from 0.03 to 0.5
- out_grad: bfloat16 [4096, 1024], P(('rep', 'ep')), may hold values from -4 to 4
- gate_weight: bfloat16 [16, 1024, 384], P('ep'), may hold values from -0.1875 to 0.1875
- up_weight: bfloat16 [16, 1024, 384], P('ep'), may hold values from -0.1875 to 0.1875
- down_weight: bfloat16 [16, 384, 1024], P('ep'), may hold values from -0.3125 to 0.3125
Outputs:
- layer_out: bfloat16 [4096, 1024], P(('rep', 'ep'))
- token_grad: bfloat16 [4096, 1024], P(('rep', 'ep'))
- route_grad: float32 [4096, 8], P(('rep', 'ep'))
- gate_weight_grad: float32 [16, 1024, 384], P('ep', 'rep')
- up_weight_grad: float32 [16, 1024, 384], P('ep', 'rep')
- down_weight_grad: float32 [16, 384, 1024], P('ep', 'rep')
Inputs may be any that keep to these rules, and one draw needn't show every extreme that they name: `expert_ids`: each row names 8 different experts. Among the rows of one device (an aligned block of 128 rows) no expert is named more than 96 times, and in every draw some expert is named exactly 96 times by the rows of some device.
All inputs are finite; a program needn't handle non-finite values.
Results may differ from a plain program's by a relative error of at most 0.014.
Values may be sent and summed in bfloat16 or wider, within the bound.
No kernel may reach another device: no remote copies, remote signals or barrier semaphores. Data moves between devices by JAX's collectives and lax.ppermute only.
A program may use at most 128 MiB of HBM per device.

v0:
```python
import jax
import jax.numpy as jnp
from jax import lax
from jax.sharding import PartitionSpec as P


def silu_parts(gate_pre):
    sigmoid_gate = jax.nn.sigmoid(gate_pre)
    return (gate_pre * sigmoid_gate, sigmoid_gate * (1.0 + gate_pre * (1.0 - sigmoid_gate)))


def expert_forward(expert_in, gate_weight, up_weight, down_weight):
    gate_pre = jnp.einsum(
        "esnd,edf->esnf", expert_in, gate_weight, preferred_element_type=jnp.float32
    )
    up_pre = jnp.einsum("esnd,edf->esnf", expert_in, up_weight, preferred_element_type=jnp.float32)
    silu_gate, silu_slope = silu_parts(gate_pre)
    hidden = (silu_gate * up_pre).astype(jnp.bfloat16)
    expert_out = jnp.einsum(
        "esnf,efd->esnd", hidden, down_weight, preferred_element_type=jnp.float32
    ).astype(jnp.bfloat16)
    return (gate_pre, up_pre, hidden, expert_out)


def expert_backward(out_rows, gate_pre, up_pre, gate_weight, up_weight, down_weight):
    hidden_grad = jnp.einsum(
        "esnd,efd->esnf", out_rows, down_weight, preferred_element_type=jnp.float32
    )
    silu_gate, silu_slope = silu_parts(gate_pre)
    gate_delta = (hidden_grad * up_pre * silu_slope).astype(jnp.bfloat16)
    up_delta = (hidden_grad * silu_gate).astype(jnp.bfloat16)
    in_grads = jnp.einsum(
        "esnf,edf->esnd", gate_delta, gate_weight, preferred_element_type=jnp.float32
    ) + jnp.einsum("esnf,edf->esnd", up_delta, up_weight, preferred_element_type=jnp.float32)
    return (gate_delta, up_delta, in_grads.astype(jnp.bfloat16))


def per_device(tokens, expert_ids, route_weights, out_grad, gate_weight, up_weight, down_weight):
    tok_rows, model_width = tokens.shape
    top_count = expert_ids.shape[1]
    local_experts = gate_weight.shape[0]
    peer_count = lax.axis_size("ep")
    experts = local_experts * peer_count
    capacity = 3 * tok_rows * top_count // (2 * experts)
    slot_total = local_experts * peer_count * capacity
    flat_ids = expert_ids.reshape(-1)
    columns = jnp.arange(experts, dtype=jnp.int32)
    onehot = (flat_ids[:, None] == columns[None, :]).astype(jnp.int32)
    slot_rank = jnp.sum((jnp.cumsum(onehot, axis=0) - 1) * onehot, axis=1)
    target = (
        flat_ids % local_experts * peer_count + flat_ids // local_experts
    ) * capacity + slot_rank
    source = jnp.arange(tok_rows * top_count, dtype=jnp.int32) // top_count

    def pack_rows(pair_rows):
        filled = jnp.zeros((slot_total, model_width), jnp.bfloat16).at[target].set(pair_rows)
        return filled.reshape(local_experts, peer_count, capacity, model_width)

    def unpack_rows(returned):
        return returned.reshape(slot_total, model_width)[target].reshape(
            tok_rows, top_count, model_width
        )

    sent_tokens = pack_rows(tokens[source])
    scaled = (route_weights[:, :, None] * out_grad[:, None, :]).astype(jnp.bfloat16)
    sent_grads = pack_rows(scaled.reshape(tok_rows * top_count, model_width))
    expert_in = lax.all_to_all(sent_tokens, "ep", split_axis=1, concat_axis=1, tiled=True)
    gate_pre, up_pre, hidden, expert_out = expert_forward(
        expert_in, gate_weight, up_weight, down_weight
    )
    returned = lax.all_to_all(expert_out, "ep", split_axis=1, concat_axis=1, tiled=True)
    returned, expert_in, gate_pre, up_pre, hidden = (returned, expert_in, gate_pre, up_pre, hidden)
    out_rows = lax.all_to_all(sent_grads, "ep", split_axis=1, concat_axis=1, tiled=True)
    gate_delta, up_delta, in_grads = expert_backward(
        out_rows, gate_pre, up_pre, gate_weight, up_weight, down_weight
    )
    in_returned = lax.all_to_all(in_grads, "ep", split_axis=1, concat_axis=1, tiled=True)
    grad_down = jnp.einsum("esnf,esnd->efd", hidden, out_rows, preferred_element_type=jnp.float32)
    grad_gate = jnp.einsum(
        "esnd,esnf->edf", expert_in, gate_delta, preferred_element_type=jnp.float32
    )
    grad_up = jnp.einsum("esnd,esnf->edf", expert_in, up_delta, preferred_element_type=jnp.float32)
    down_share = lax.psum_scatter(
        grad_down.astype(jnp.bfloat16), "rep", scatter_dimension=1, tiled=True
    ).astype(jnp.float32)
    gate_share, up_share = (
        lax.psum_scatter(
            grad_gate.astype(jnp.bfloat16), "rep", scatter_dimension=1, tiled=True
        ).astype(jnp.float32),
        lax.psum_scatter(
            grad_up.astype(jnp.bfloat16), "rep", scatter_dimension=1, tiled=True
        ).astype(jnp.float32),
    )
    out_pairs = unpack_rows(returned)
    layer_out = jnp.sum(route_weights[:, :, None] * out_pairs, axis=1).astype(jnp.bfloat16)
    route_grad = jnp.einsum("td,tkd->tk", out_grad, out_pairs, preferred_element_type=jnp.float32)
    token_grad = jnp.sum(unpack_rows(in_returned).astype(jnp.float32), axis=1).astype(jnp.bfloat16)
    return (layer_out, token_grad, route_grad, gate_share, up_share, down_share)


def solution(mesh):
    return jax.shard_map(
        per_device,
        mesh=mesh,
        in_specs=(
            P(("rep", "ep"), None),
            P(("rep", "ep"), None),
            P(("rep", "ep"), None),
            P(("rep", "ep"), None),
            P("ep", None, None),
            P("ep", None, None),
            P("ep", None, None),
        ),
        out_specs=(
            P(("rep", "ep"), None),
            P(("rep", "ep"), None),
            P(("rep", "ep"), None),
            P("ep", "rep", None),
            P("ep", "rep", None),
            P("ep", "rep", None),
        ),
        check_vma=False,
    )
```

profile of v0, /device:TPU:0, one launch (start us, length us, event | category | flops | bytes accessed | tf_op | source)
XLA Modules:
  0.0 370.3 jit_solution(16945968723066475624)
XLA Ops:
  7.2 0.0 copy-start
  7.2 0.9 copy.41
  8.1 0.1 eq.31
  8.2 0.1 eq.27
  8.3 0.1 reshape.221
  8.4 4.5 %reduce-window.6 = s32[16,8,128]{2,1,0:T(8,128)S(1)} reduce-window(s32[16,8,128]{2,1,0:T(8,128)S(1)} %fusion.34, s32[]{:T(128)} %constant.50.clone.1), window={size=1x1x128 pad=0_0x0_0x127_0}, to_apply=%region_0.0 | reduce-window | flops 2080768 | bytes 131076 | tf_op jit(solution)/shard_map/reduce-window
  12.9 0.1 slice.14
  13.0 0.1 copy.44
  13.2 0.1 copy.45
  13.2 0.1 add_add_fusion
  13.4 17.0 %scatter_custom_fusion = bf16[1536,1024]{1,0:T(8,128)(2,1)} fusion(s32[1024]{0:T(1024)S(1)} %bitcast.80, bf16[128,1024]{1,0:T(8,128)(2,1)} %param.7, s32[1024]{0:T(1024)S(1)} %broadcast_clamp_fusion.1, bf16[]{:T(256)} %constant.49.clone.1), kind=kCustom, calls=%fused_computation.30 | custom fusion | bytes 3146240 | tf_op jit(solution)/shard_map/scatter | solution.py:56
  30.4 4.0 %copy.46 = bf16[2,8,96,1024]{3,2,0,1:T(8,128)(2,1)} copy(bf16[2,8,96,1024]{3,2,1,0:T(8,128)(2,1)} %bitcast.75) | data formatting | bytes 6291456 | tf_op jit(solution)/shard_map/reshape | solution.py:57
  34.4 7.4 %all-to-all-start = ((bf16[2,8,96,1024]{3,2,0,1:T(8,128)(2,1)}), bf16[2,8,96,1024]{3,2,0,1:T(8,128)(2,1)}, u32[]{:S(2)}, u32[]{:S(2)}) async-start(bf16[2,8,96,1024]{3,2,0,1:T(8,128)(2,1)} %copy.46), calls=%async_computation | async-start | bytes 6291456 | tf_op jit(solution)/shard_map/all_to_all | solution.py:67
  41.8 0.0 copy-done.9
  41.9 0.1 copy.40
  42.0 0.1 mul.86
  42.0 0.0 copy-done.8
  42.1 7.8 %scatter_custom_fusion.1 = bf16[1536,1024]{1,0:T(8,128)(2,1)} fusion(s32[1024]{0:T(1024)S(1)} %bitcast.81, f32[128,1024]{1,0:T(8,128)S(1)} %convert_element_type.59, f32[1024]{0:T(1024)S(1)} %mul.86, bf16[]{:T(256)} %constant.49.clone.1), kind=kCustom, calls=%fused_computation.26 | custom fusion | flops 2097152 | bytes 3674114 | tf_op jit(solution)/shard_map/scatter | solution.py:56
  49.9 3.9 %copy.52 = bf16[2,8,96,1024]{3,2,0,1:T(8,128)(2,1)} copy(bf16[2,8,96,1024]{3,2,1,0:T(8,128)(2,1)} %bitcast.74) | data formatting | bytes 6291456 | tf_op jit(solution)/shard_map/reshape | solution.py:57
  53.9 58.8 %all-to-all-done = bf16[2,8,96,1024]{3,2,0,1:T(8,128)(2,1)} async-done(((bf16[2,8,96,1024]{3,2,0,1:T(8,128)(2,1)}), bf16[2,8,96,1024]{3,2,0,1:T(8,128)(2,1)}, u32[]{:S(2)}, u32[]{:S(2)}) %all-to-all-start) | async-done | bytes 3145760 | tf_op jit(solution)/shard_map/all_to_all | solution.py:67
  112.7 4.5 %all-to-all-start.2 = ((bf16[2,8,96,1024]{3,2,0,1:T(8,128)(2,1)}), bf16[2,8,96,1024]{3,2,0,1:T(8,128)(2,1)}, u32[]{:S(2)}, u32[]{:S(2)}) async-start(bf16[2,8,96,1024]{3,2,0,1:T(8,128)(2,1)} %copy.52), calls=%async_computation.2 | async-start | bytes 6291456 | tf_op jit(solution)/shard_map/all_to_all | solution.py:73
  117.1 0.0 copy-done.2
  117.1 0.0 copy-start.3
  117.2 5.2 %fusion.5 = f32[2,8,96,384]{3,2,1,0:T(8,128)} fusion(bf16[2,8,96,1024]{3,2,0,1:T(8,128)(2,1)} %all-to-all-done, bf16[2,1024,384]{2,1,0:T(8,128)(2,1)S(1)} %copy-done.2), kind=kOutput, calls=%fused_computation.16 | convolution fusion | flops 1207959552 | bytes 7077888 | tf_op jit(solution)/shard_map/esnd,edf->esnf/dot_general | solution.py:16
  122.4 0.0 copy-done.3
  122.4 5.1 %fusion.7 = f32[2,8,96,384]{3,2,1,0:T(8,128)} fusion(bf16[2,8,96,1024]{3,2,0,1:T(8,128)(2,1)} %all-to-all-done, bf16[2,1024,384]{2,1,0:T(8,128)(2,1)S(1)} %copy-done.3), kind=kOutput, calls=%fused_computation.18 | convolution fusion | flops 1207959552 | bytes 7077888 | tf_op jit(solution)/shard_map/esnd,edf->esnf/dot_general | solution.py:13
  127.5 59.8 %all-to-all-done.2 = bf16[2,8,96,1024]{3,2,0,1:T(8,128)(2,1)} async-done(((bf16[2,8,96,1024]{3,2,0,1:T(8,128)(2,1)}), bf16[2,8,96,1024]{3,2,0,1:T(8,128)(2,1)}, u32[]{:S(2)}, u32[]{:S(2)}) %all-to-all-start.2) | async-done | bytes 3145760 | tf_op jit(solution)/shard_map/all_to_all | solution.py:73
  187.3 0.0 copy-done
  187.3 7.2 %multiply_convert_fusion = (bf16[2,8,96,384]{3,2,1,0:T(8,128)(2,1)}, bf16[2,8,96,384]{3,2,1,0:T(8,128)(2,1)}, bf16[2,8,96,384]{3,2,1,0:T(8,128)(2,1)S(1)}) fusion(f32[2,8,96,384]{3,2,1,0:T(8,128)} %fusion.7, f32[2,8,96,384]{3,2,1,0:T(8,128)} %fusion.5, bf16[2,384,1024]{2,1,0:T(8,128)(2,1)S(1)} %copy-done, bf16[2,8,96,1024]{3,2,0,1:T(8,128)(2,1)} %all-to-all-done.2), kind=kOutput, calls=%fused_computation.20 | convolution fusion | flops 1216806912 | bytes 12976128 | tf_op jit(solution)/shard_map/esnd,efd->esnf/dot_general | solution.py:26
  194.5 1.8 convolution_convert_fusion
  196.3 0.0 copy-done.10
  196.3 2.1 copy.49
  198.4 4.5 %all-to-all-start.1 = ((bf16[2,8,96,1024]{3,2,0,1:T(8,128)(2,1)}), bf16[2,8,96,1024]{3,2,0,1:T(8,128)(2,1)}, u32[]{:S(2)}, u32[]{:S(2)}) async-start(bf16[2,8,96,1024]{3,2,0,1:T(8,128)(2,1)} %copy.49), calls=%async_computation.1 | async-start | bytes 6291456 | tf_op jit(solution)/shard_map/all_to_all | solution.py:71
  202.9 0.3 reduce-scatter.8.cloned.1.call-start
  203.2 4.9 %bitcast_convert_fusion = bf16[2,384,1024]{2,1,0:T(8,128)(2,1)} fusion(bf16[2,8,96,384]{3,2,1,0:T(8,128)(2,1)} %copy-done.10, bf16[2,8,96,1024]{3,2,0,1:T(8,128)(2,1)} %all-to-all-done.2), kind=kOutput, calls=%fused_computation.9 | convolution fusion | flops 1208745984 | bytes 5898240 | tf_op jit(solution)/shard_map/esnf,esnd->efd/dot_general | solution.py:78
  208.0 0.0 reduce-scatter.8.cloned.1.call-update
  208.1 0.0 reduce-scatter.6.cloned.1.call-start
  208.1 4.9 %bitcast_convert_fusion.1 = bf16[2,1024,384]{2,1,0:T(8,128)(2,1)} fusion(bf16[2,8,96,1024]{3,2,0,1:T(8,128)(2,1)} %all-to-all-done, bf16[2,8,96,384]{3,2,1,0:T(8,128)(2,1)S(1)} %copy-done.6), kind=kOutput, calls=%fused_computation.10 | convolution fusion | flops 1208745984 | bytes 5898240 | tf_op jit(solution)/shard_map/esnd,esnf->edf/dot_general | solution.py:82
  213.0 0.0 reduce-scatter.6.cloned.1.call-update
  213.1 1.4 copy-done.4
  214.4 3.2 fusion.22
  217.6 0.0 copy-done.7
  217.7 1.8 add_convert_fusion
  219.5 1.9 copy.54
  221.4 51.6 %all-to-all-done.1 = bf16[2,8,96,1024]{3,2,0,1:T(8,128)(2,1)} async-done(((bf16[2,8,96,1024]{3,2,0,1:T(8,128)(2,1)}), bf16[2,8,96,1024]{3,2,0,1:T(8,128)(2,1)}, u32[]{:S(2)}, u32[]{:S(2)}) %all-to-all-start.1) | async-done | bytes 3145760 | tf_op jit(solution)/shard_map/all_to_all | solution.py:71
  273.1 4.5 %all-to-all-start.3 = ((bf16[2,8,96,1024]{3,2,0,1:T(8,128)(2,1)}), bf16[2,8,96,1024]{3,2,0,1:T(8,128)(2,1)}, u32[]{:S(2)}, u32[]{:S(2)}) async-start(bf16[2,8,96,1024]{3,2,0,1:T(8,128)(2,1)} %copy.54), calls=%async_computation.3 | async-start | bytes 6291456 | tf_op jit(solution)/shard_map/all_to_all | solution.py:77
  277.5 0.3 reduce-scatter.4.cloned.1.call-start
  277.8 4.9 %bitcast_convert_fusion.2 = bf16[2,1024,384]{2,1,0:T(8,128)(2,1)} fusion(bf16[2,8,96,1024]{3,2,0,1:T(8,128)(2,1)} %all-to-all-done, bf16[2,8,96,384]{3,2,1,0:T(8,128)(2,1)S(1)} %copy-done.5), kind=kOutput, calls=%fused_computation.11 | convolution fusion | flops 1208745984 | bytes 5898240 | tf_op jit(solution)/shard_map/esnd,esnf->edf/dot_general | solution.py:79
  282.8 0.0 reduce-scatter.4.cloned.1.call-update
  282.8 0.0 reduce-scatter.8.cloned.1.call-done
  282.8 2.0 convert_element_type.69
  284.8 1.9 convert_element_type.67
  286.7 25.3 %reduce-scatter.4.cloned.1.call-done = bf16[2,256,384]{2,1,0:T(8,128)(2,1)} async-done(((bf16[2,1024,384]{2,1,0:T(8,128)(2,1)}), bf16[2,256,384]{2,1,0:T(8,128)(2,1)}) %reduce-scatter.4.cloned.1.call-update) | async-done | bytes 393232 | tf_op jit(solution)/shard_map/reduce_scatter | solution.py:87
  312.0 1.9 convert_element_type.65
  313.9 4.0 %copy.50 = bf16[2,8,96,1024]{3,2,1,0:T(8,128)(2,1)} copy(bf16[2,8,96,1024]{3,2,0,1:T(8,128)(2,1)} %all-to-all-done.1) | data formatting | bytes 6291456 | tf_op jit(solution)/shard_map/all_to_all | solution.py:71
  317.9 8.3 %gather_fusion = bf16[1024,1024]{1,0:T(8,128)(2,1)} fusion(bf16[1536,1024]{1,0:T(8,128)(2,1)} %bitcast.73, s32[1024]{0:T(1024)S(1)} %broadcast_clamp_fusion), kind=kCustom, calls=%fused_computation.1 | custom fusion | bytes 4198400 | tf_op jit(solution)/shard_map/gather | solution.py:60
  326.2 2.8 fusion.12
  329.0 0.7 copy.63
  329.7 3.7 multiply_reduce_fusion
  333.3 14.4 %all-to-all-done.3 = bf16[2,8,96,1024]{3,2,0,1:T(8,128)(2,1)} async-done(((bf16[2,8,96,1024]{3,2,0,1:T(8,128)(2,1)}), bf16[2,8,96,1024]{3,2,0,1:T(8,128)(2,1)}, u32[]{:S(2)}, u32[]{:S(2)}) %all-to-all-start.3) | async-done | bytes 3145760 | tf_op jit(solution)/shard_map/all_to_all | solution.py:77
  347.7 4.0 %copy.55 = bf16[2,8,96,1024]{3,2,1,0:T(8,128)(2,1)} copy(bf16[2,8,96,1024]{3,2,0,1:T(8,128)(2,1)} %all-to-all-done.3) | data formatting | bytes 6291456 | tf_op jit(solution)/shard_map/all_to_all | solution.py:77
  351.7 8.4 %gather_fusion.1 = bf16[1024,1024]{1,0:T(8,128)(2,1)} fusion(bf16[1536,1024]{1,0:T(8,128)(2,1)} %bitcast.72, s32[1024]{0:T(1024)S(1)} %broadcast_clamp_fusion), kind=kCustom, calls=%fused_computation.2 | custom fusion | bytes 4198400 | tf_op jit(solution)/shard_map/gather | solution.py:60
  360.1 3.7 %bitcast_reduce_fusion = bf16[128,1024]{1,0:T(8,128)(2,1)} fusion(bf16[1024,1024]{1,0:T(8,128)(2,1)} %gather_fusion.1), kind=kLoop, calls=%fused_computation.27 | loop fusion | flops 917504 | bytes 2359296 | tf_op jit(solution)/shard_map/reduce_sum | solution.py:97
  363.8 0.0 copy-done.1
  (21 shorter events, 0.2 us)
Async XLA Ops:
  7.2 180.1 %copy-start = (bf16[2,384,1024]{2,1,0:T(8,128)(2,1)S(1)}, bf16[2,384,1024]{2,1,0:T(8,128)(2,1)}, u32[]{:S(2)}) copy-start(bf16[2,384,1024]{2,1,0:T(8,128)(2,1)} %param.13) | copy-start | bytes 4718596
  34.4 7.4 %copy-start.9 = (f32[128,8]{0,1:T(8,128)S(1)}, f32[128,8]{0,1:T(8,128)}, u32[]{:S(2)}) copy-start(f32[128,8]{0,1:T(8,128)} %param.9) | copy-start | bytes 12292
  34.4 7.6 %copy-start.8 = (bf16[128,1024]{1,0:T(8,128)(2,1)S(1)}, bf16[128,1024]{1,0:T(8,128)(2,1)}, u32[]{:S(2)}) copy-start(bf16[128,1024]{1,0:T(8,128)(2,1)} %param.10) | copy-start | bytes 786436
  34.4 78.2 %all-to-all-start = ((bf16[2,8,96,1024]{3,2,0,1:T(8,128)(2,1)}), bf16[2,8,96,1024]{3,2,0,1:T(8,128)(2,1)}, u32[]{:S(2)}, u32[]{:S(2)}) async-start(bf16[2,8,96,1024]{3,2,0,1:T(8,128)(2,1)} %copy.46), calls=%async_computation | async-start | bytes 6291456 | tf_op jit(solution)/shard_map/all_to_all | solution.py:67
  53.9 63.3 %copy-start.2 = (bf16[2,1024,384]{2,1,0:T(8,128)(2,1)S(1)}, bf16[2,1024,384]{2,1,0:T(8,128)(2,1)}, u32[]{:S(2)}) copy-start(bf16[2,1024,384]{2,1,0:T(8,128)(2,1)} %param.12) | copy-start | bytes 4718596
  112.7 74.6 %all-to-all-start.2 = ((bf16[2,8,96,1024]{3,2,0,1:T(8,128)(2,1)}), bf16[2,8,96,1024]{3,2,0,1:T(8,128)(2,1)}, u32[]{:S(2)}, u32[]{:S(2)}) async-start(bf16[2,8,96,1024]{3,2,0,1:T(8,128)(2,1)} %copy.52), calls=%async_computation.2 | async-start | bytes 6291456 | tf_op jit(solution)/shard_map/all_to_all | solution.py:73
  117.1 5.2 %copy-start.3 = (bf16[2,1024,384]{2,1,0:T(8,128)(2,1)S(1)}, bf16[2,1024,384]{2,1,0:T(8,128)(2,1)}, u32[]{:S(2)}) copy-start(bf16[2,1024,384]{2,1,0:T(8,128)(2,1)} %param.11) | copy-start | bytes 4718596
  194.5 1.8 copy-start.10
  198.4 74.6 %all-to-all-start.1 = ((bf16[2,8,96,1024]{3,2,0,1:T(8,128)(2,1)}), bf16[2,8,96,1024]{3,2,0,1:T(8,128)(2,1)}, u32[]{:S(2)}, u32[]{:S(2)}) async-start(bf16[2,8,96,1024]{3,2,0,1:T(8,128)(2,1)} %copy.49), calls=%async_computation.1 | async-start | bytes 6291456 | tf_op jit(solution)/shard_map/all_to_all | solution.py:71
  202.9 5.2 %copy-start.6 = (bf16[2,8,96,384]{3,2,1,0:T(8,128)(2,1)S(1)}, bf16[2,8,96,384]{3,2,1,0:T(8,128)(2,1)}, u32[]{:S(2)}) copy-start(bf16[2,8,96,384]{3,2,1,0:T(8,128)(2,1)} %get-tuple-element.6) | copy-start | bytes 3538948
  202.9 79.9 %reduce-scatter.8.cloned.1.call-start = ((), (), s32[]{:S(2)}) async-start(), calls=%async_computation.9 | async-start | bytes 1966080 | tf_op jit(solution)/shard_map/reduce_scatter | solution.py:83
  208.1 76.7 %reduce-scatter.6.cloned.1.call-start = ((), (), s32[]{:S(2)}) async-start(), calls=%async_computation.8 | async-start | bytes 1966080 | tf_op jit(solution)/shard_map/reduce_scatter | solution.py:90
  213.0 1.4 copy-start.4
  214.4 3.2 copy-start.7
  221.4 56.4 %copy-start.5 = (bf16[2,8,96,384]{3,2,1,0:T(8,128)(2,1)S(1)}, bf16[2,8,96,384]{3,2,1,0:T(8,128)(2,1)}, u32[]{:S(2)}) copy-start(bf16[2,8,96,384]{3,2,1,0:T(8,128)(2,1)} %get-tuple-element.7) | copy-start | bytes 3538948
  273.1 74.6 %all-to-all-start.3 = ((bf16[2,8,96,1024]{3,2,0,1:T(8,128)(2,1)}), bf16[2,8,96,1024]{3,2,0,1:T(8,128)(2,1)}, u32[]{:S(2)}, u32[]{:S(2)}) async-start(bf16[2,8,96,1024]{3,2,0,1:T(8,128)(2,1)} %copy.54), calls=%async_computation.3 | async-start | bytes 6291456 | tf_op jit(solution)/shard_map/all_to_all | solution.py:77
  277.5 34.5 %reduce-scatter.4.cloned.1.call-start = ((), (), s32[]{:S(2)}) async-start(), calls=%async_computation.7 | async-start | bytes 1966080 | tf_op jit(solution)/shard_map/reduce_scatter | solution.py:87
  351.6 12.2 %copy-start.1 = (bf16[2,384,1024]{2,1,0:T(8,128)(2,1)S(1)}, bf16[2,384,1024]{2,1,0:T(8,128)(2,1)}, u32[]{:S(2)}) copy-start(bf16[2,384,1024]{2,1,0:T(8,128)(2,1)} %param.13) | copy-start | bytes 4718596
Sparse Core Ops, SparseCore 0:
  208.2 29.1 reduce-scatter.7
  239.9 28.0 reduce-scatter.5
  282.9 29.0 reduce-scatter.3
where the time goes:
time: 372 us; the launch traced here: 370 us
  waiting for transfers between devices  210 us (56%)
  local copies, waits for them, and re-layouts  57.4 us (15%)
  matrix products  41.9 us (11%)
  other arithmetic  25.8 us (7%)
  starting transfers between devices  21.4 us (6%)
  between operations  14 us (4%)
    all_to_all x1, waiting for transfers between devices, per_device(): lax.all_to_all(sent_grads, 'ep', split_axis=1, concat_axis=1, tiled=True)  59.8 us
    all_to_all x1, waiting for transfers between devices, per_device(): lax.all_to_all(sent_tokens, 'ep', split_axis=1, concat_axis=1, tiled=True)  58.8 us
    all_to_all x1, waiting for transfers between devices, per_device(): lax.all_to_all(expert_out, 'ep', split_axis=1, concat_axis=1, tiled=True)  51.6 us
    reduce_scatter x1, waiting for transfers between devices, per_device(): lax.psum_scatter(grad_gate.astype(jnp.bfloat16), 'rep', scatter_dimension...  25.3 us
    scatter x1, local copies, waits for them, and re-layouts, pack_rows(): jnp.zeros((slot_total, model_width), jnp.bfloat16).at[target].set(pair_rows)  17 us
    gather x2, local copies, waits for them, and re-layouts, unpack_rows(): returned.reshape(slot_total, model_width)[target]  16.7 us
    all_to_all x1, waiting for transfers between devices, per_device(): lax.all_to_all(in_grads, 'ep', split_axis=1, concat_axis=1, tiled=True)  14.4 us
    reshape x2, local copies, waits for them, and re-layouts, pack_rows(): return filled.reshape(local_experts, peer_count, capacity, model_width)  7.93 us
  transfers between devices with their start and end apart: 7, of which 5 were waited for; matrix products, arithmetic and copies ran while one was open for 19% of the time, Pallas kernels for 0%

commit v1 on v0

--- a/solution.py
+++ b/solution.py
@@ -74,7 +74,10 @@
     gate_delta, up_delta, in_grads = expert_backward(
         out_rows, gate_pre, up_pre, gate_weight, up_weight, down_weight
     )
-    in_returned = lax.all_to_all(in_grads, "ep", split_axis=1, concat_axis=1, tiled=True)
+    in_returned = jnp.concatenate(
+        lax.all_to_all(jnp.stack(jnp.split(in_grads, lax.axis_size("ep"), axis=1)), "ep", 0, 0),
+        axis=1,
+    )
     grad_down = jnp.einsum("esnf,esnd->efd", hidden, out_rows, preferred_element_type=jnp.float32)
     grad_gate = jnp.einsum(
         "esnd,esnf->edf", expert_in, gate_delta, preferred_element_type=jnp.float32

time: 372 us -> 378 us (1.016)
  local copies, waits for them, and re-layouts: 57.4 us -> 62.8 us
    unnamed x24 -> x31, local copies, waits for them, and re-layouts: 2.44 us -> 9.11 us
    all_to_all x1 -> x0, local copies, waits for them, and re-layouts: 3.96 us -> none  [per_device(): lax.all_to_all(in_grads, 'ep', split_axis=1, concat_axis=1, tiled=True)]
    reshape x0 -> x1, local copies, waits for them, and re-layouts: none -> 3.96 us  [per_device(): jnp.concatenate(lax.all_to_all(jnp.stack(jnp.split(in_grads, lax.axis_siz...]
  transfers between devices with their start and end apart: 7 -> 7, of which waited for: 5 -> 5; matrix products, arithmetic and copies ran while one was open for 19% -> 20% of each run, Pallas kernels for 0% -> 0%
where the time goes in v1:
time: 378 us; the launch traced here: 377 us
  waiting for transfers between devices  210 us (56%)
  local copies, waits for them, and re-layouts  62.8 us (17%)
  matrix products  42.7 us (11%)
  other arithmetic  25.7 us (7%)
  starting transfers between devices  21.8 us (6%)
  between operations  13.9 us (4%)
    all_to_all x1, waiting for transfers between devices, per_device(): lax.all_to_all(sent_grads, 'ep', split_axis=1, concat_axis=1, tiled=True)  59.5 us
    all_to_all x1, waiting for transfers between devices, per_device(): lax.all_to_all(sent_tokens, 'ep', split_axis=1, concat_axis=1, tiled=True)  58.8 us
    all_to_all x1, waiting for transfers between devices, per_device(): lax.all_to_all(expert_out, 'ep', split_axis=1, concat_axis=1, tiled=True)  52.1 us
    reduce_scatter x1, waiting for transfers between devices, per_device(): lax.psum_scatter(grad_gate.astype(jnp.bfloat16), 'rep', scatter_dimension...  25.3 us
    scatter x1, local copies, waits for them, and re-layouts, pack_rows(): jnp.zeros((slot_total, model_width), jnp.bfloat16).at[target].set(pair_rows)  16.8 us
    gather x2, local copies, waits for them, and re-layouts, unpack_rows(): returned.reshape(slot_total, model_width)[target]  16.7 us
    all_to_all x1, waiting for transfers between devices, per_device(): lax.all_to_all(jnp.stack(jnp.split(in_grads, lax.axis_size('ep'), axis=1)...  14.4 us
    unnamed x31, local copies, waits for them, and re-layouts  9.11 us
  transfers between devices with their start and end apart: 7, of which 5 were waited for; matrix products, arithmetic and copies ran while one was open for 20% of the time, Pallas kernels for 0%

profile of v1, /device:TPU:0, one launch (start us, length us, event | category | flops | bytes accessed | tf_op | source)
XLA Modules:
  0.0 377.1 jit_solution(9531456855052737407)
XLA Ops:
  7.2 0.0 copy-start
  7.2 0.9 copy.62
  8.1 0.1 eq.31
  8.2 0.1 eq.27
  8.3 0.1 reshape.221
  8.4 4.5 %reduce-window.6 = s32[16,8,128]{2,1,0:T(8,128)S(1)} reduce-window(s32[16,8,128]{2,1,0:T(8,128)S(1)} %fusion.42, s32[]{:T(128)} %constant.50.clone.1), window={size=1x1x128 pad=0_0x0_0x127_0}, to_apply=%region_0.0 | reduce-window | flops 2080768 | bytes 131076 | tf_op jit(solution)/shard_map/reduce-window
  12.9 0.1 slice.14
  13.0 0.1 copy.65
  13.2 0.1 copy.66
  13.2 0.1 add_add_fusion
  13.4 16.8 %scatter_custom_fusion = bf16[1536,1024]{1,0:T(8,128)(2,1)} fusion(s32[1024]{0:T(1024)S(1)} %bitcast.127, bf16[128,1024]{1,0:T(8,128)(2,1)} %param.7, s32[1024]{0:T(1024)S(1)} %broadcast_clamp_fusion.1, bf16[]{:T(256)} %constant.49.clone.1), kind=kCustom, calls=%fused_computation.30 | custom fusion | bytes 3146240 | tf_op jit(solution)/shard_map/scatter | solution.py:56
  30.2 4.0 %copy.67 = bf16[2,8,96,1024]{3,2,0,1:T(8,128)(2,1)} copy(bf16[2,8,96,1024]{3,2,1,0:T(8,128)(2,1)} %bitcast.122) | data formatting | bytes 6291456 | tf_op jit(solution)/shard_map/reshape | solution.py:57
  34.2 7.4 %all-to-all-start = ((bf16[2,8,96,1024]{3,2,0,1:T(8,128)(2,1)}), bf16[2,8,96,1024]{3,2,0,1:T(8,128)(2,1)}, u32[]{:S(2)}, u32[]{:S(2)}) async-start(bf16[2,8,96,1024]{3,2,0,1:T(8,128)(2,1)} %copy.67), calls=%async_computation | async-start | bytes 6291456 | tf_op jit(solution)/shard_map/all_to_all | solution.py:67
  41.6 0.1 copy.61
  41.7 0.1 mul.86
  41.9 7.8 %scatter_custom_fusion.1 = bf16[1536,1024]{1,0:T(8,128)(2,1)} fusion(s32[1024]{0:T(1024)S(1)} %bitcast.128, f32[128,1024]{1,0:T(8,128)S(1)} %convert_element_type.59, f32[1024]{0:T(1024)S(1)} %mul.86, bf16[]{:T(256)} %constant.49.clone.1), kind=kCustom, calls=%fused_computation.26 | custom fusion | flops 2097152 | bytes 3674114 | tf_op jit(solution)/shard_map/scatter | solution.py:56
  49.6 4.0 %copy.73 = bf16[2,8,96,1024]{3,2,0,1:T(8,128)(2,1)} copy(bf16[2,8,96,1024]{3,2,1,0:T(8,128)(2,1)} %bitcast.121) | data formatting | bytes 6291456 | tf_op jit(solution)/shard_map/reshape | solution.py:57
  53.6 58.8 %all-to-all-done = bf16[2,8,96,1024]{3,2,0,1:T(8,128)(2,1)} async-done(((bf16[2,8,96,1024]{3,2,0,1:T(8,128)(2,1)}), bf16[2,8,96,1024]{3,2,0,1:T(8,128)(2,1)}, u32[]{:S(2)}, u32[]{:S(2)}) %all-to-all-start) | async-done | bytes 3145760 | tf_op jit(solution)/shard_map/all_to_all | solution.py:67
  112.4 4.5 %all-to-all-start.2 = ((bf16[2,8,96,1024]{3,2,0,1:T(8,128)(2,1)}), bf16[2,8,96,1024]{3,2,0,1:T(8,128)(2,1)}, u32[]{:S(2)}, u32[]{:S(2)}) async-start(bf16[2,8,96,1024]{3,2,0,1:T(8,128)(2,1)} %copy.73), calls=%async_computation.2 | async-start | bytes 6291456 | tf_op jit(solution)/shard_map/all_to_all | solution.py:73
  116.9 0.3 reduce-scatter.8.cloned.1.call-start
  117.2 0.0 copy-start.3
  117.2 5.3 %fusion.5 = f32[2,8,96,384]{3,2,1,0:T(8,128)} fusion(bf16[2,8,96,1024]{3,2,0,1:T(8,128)(2,1)} %all-to-all-done, bf16[2,1024,384]{2,1,0:T(8,128)(2,1)S(1)} %copy-done.2), kind=kOutput, calls=%fused_computation.16 | convolution fusion | flops 1207959552 | bytes 7077888 | tf_op jit(solution)/shard_map/esnd,edf->esnf/dot_general | solution.py:16
  122.5 5.1 %fusion.7 = f32[2,8,96,384]{3,2,1,0:T(8,128)} fusion(bf16[2,8,96,1024]{3,2,0,1:T(8,128)(2,1)} %all-to-all-done, bf16[2,1024,384]{2,1,0:T(8,128)(2,1)S(1)} %copy-done.3), kind=kOutput, calls=%fused_computation.18 | convolution fusion | flops 1207959552 | bytes 7077888 | tf_op jit(solution)/shard_map/esnd,edf->esnf/dot_general | solution.py:13
  127.6 59.5 %all-to-all-done.2 = bf16[2,8,96,1024]{3,2,0,1:T(8,128)(2,1)} async-done(((bf16[2,8,96,1024]{3,2,0,1:T(8,128)(2,1)}), bf16[2,8,96,1024]{3,2,0,1:T(8,128)(2,1)}, u32[]{:S(2)}, u32[]{:S(2)}) %all-to-all-start.2) | async-done | bytes 3145760 | tf_op jit(solution)/shard_map/all_to_all | solution.py:73
  187.1 7.2 %multiply_convert_fusion = (bf16[2,8,96,384]{3,2,1,0:T(8,128)(2,1)}, bf16[2,8,96,384]{3,2,1,0:T(8,128)(2,1)}, bf16[2,8,96,384]{3,2,1,0:T(8,128)(2,1)S(1)}) fusion(f32[2,8,96,384]{3,2,1,0:T(8,128)} %fusion.7, f32[2,8,96,384]{3,2,1,0:T(8,128)} %fusion.5, bf16[2,384,1024]{2,1,0:T(8,128)(2,1)S(1)} %copy-done, bf16[2,8,96,1024]{3,2,0,1:T(8,128)(2,1)} %all-to-all-done.2), kind=kOutput, calls=%fused_computation.20 | convolution fusion | flops 1216806912 | bytes 12976128 | tf_op jit(solution)/shard_map/esnd,efd->esnf/dot_general | solution.py:26
  194.2 1.0 copy-done.10
  195.3 4.5 %bitcast_convert_fusion = bf16[2,384,1024]{2,1,0:T(8,128)(2,1)} fusion(bf16[2,8,96,384]{3,2,1,0:T(8,128)(2,1)S(1)} %get-tuple-element.8, bf16[2,8,96,1024]{3,2,0,1:T(8,128)(2,1)} %all-to-all-done.2), kind=kOutput, calls=%fused_computation.9 | convolution fusion | flops 1208745984 | bytes 5898240 | tf_op jit(solution)/shard_map/esnf,esnd->efd/dot_general | solution.py:81
  199.8 0.0 reduce-scatter.8.cloned.1.call-update
  199.8 3.1 convolution_convert_fusion
  202.9 2.1 copy.70
  205.0 4.6 %all-to-all-start.1 = ((bf16[2,8,96,1024]{3,2,0,1:T(8,128)(2,1)}), bf16[2,8,96,1024]{3,2,0,1:T(8,128)(2,1)}, u32[]{:S(2)}, u32[]{:S(2)}) async-start(bf16[2,8,96,1024]{3,2,0,1:T(8,128)(2,1)} %copy.70), calls=%async_computation.1 | async-start | bytes 6291456 | tf_op jit(solution)/shard_map/all_to_all | solution.py:71
  209.6 0.3 reduce-scatter.6.cloned.1.call-start
  209.9 4.9 %bitcast_convert_fusion.1 = bf16[2,1024,384]{2,1,0:T(8,128)(2,1)} fusion(bf16[2,8,96,1024]{3,2,0,1:T(8,128)(2,1)} %all-to-all-done, bf16[2,8,96,384]{3,2,1,0:T(8,128)(2,1)S(1)} %copy-done.6), kind=kOutput, calls=%fused_computation.10 | convolution fusion | flops 1208745984 | bytes 5898240 | tf_op jit(solution)/shard_map/esnd,esnf->edf/dot_general | solution.py:85
  214.8 0.0 reduce-scatter.6.cloned.1.call-update
  214.8 1.6 copy-done.4
  216.4 3.2 fusion.22
  219.6 1.8 add_convert_fusion
  221.4 0.8 fusion.39
  222.2 0.8 fusion.38
  223.0 0.8 fusion.37
  223.8 0.8 fusion.36
  224.6 0.8 fusion.35
  225.4 0.8 fusion.34
  226.1 0.8 fusion.33
  226.9 0.8 fusion.32
  227.7 52.1 %all-to-all-done.1 = bf16[2,8,96,1024]{3,2,0,1:T(8,128)(2,1)} async-done(((bf16[2,8,96,1024]{3,2,0,1:T(8,128)(2,1)}), bf16[2,8,96,1024]{3,2,0,1:T(8,128)(2,1)}, u32[]{:S(2)}, u32[]{:S(2)}) %all-to-all-start.1) | async-done | bytes 3145760 | tf_op jit(solution)/shard_map/all_to_all | solution.py:71
  279.8 4.5 %all-to-all-start.3 = ((bf16[8,2,1,96,1024]{4,3,1,2,0:T(8,128)(2,1)}), bf16[8,2,1,96,1024]{4,3,1,2,0:T(8,128)(2,1)}, u32[]{:S(2)}, u32[]{:S(2)}) async-start(bf16[8,2,1,96,1024]{4,3,1,2,0:T(8,128)(2,1)} %fusion.32), calls=%async_computation.3 | async-start | bytes 6291456 | tf_op jit(solution)/shard_map/all_to_all | solution.py:78
  284.2 0.3 reduce-scatter.4.cloned.1.call-start
  284.6 4.9 %bitcast_convert_fusion.2 = bf16[2,1024,384]{2,1,0:T(8,128)(2,1)} fusion(bf16[2,8,96,1024]{3,2,0,1:T(8,128)(2,1)} %all-to-all-done, bf16[2,8,96,384]{3,2,1,0:T(8,128)(2,1)S(1)} %copy-done.5), kind=kOutput, calls=%fused_computation.11 | convolution fusion | flops 1208745984 | bytes 5898240 | tf_op jit(solution)/shard_map/esnd,esnf->edf/dot_general | solution.py:82
  289.5 0.0 reduce-scatter.4.cloned.1.call-update
  289.5 0.0 reduce-scatter.8.cloned.1.call-done
  289.5 2.0 convert_element_type.69
  291.5 1.9 convert_element_type.67
  293.4 25.3 %reduce-scatter.4.cloned.1.call-done = bf16[2,256,384]{2,1,0:T(8,128)(2,1)} async-done(((bf16[2,1024,384]{2,1,0:T(8,128)(2,1)}), bf16[2,256,384]{2,1,0:T(8,128)(2,1)}) %reduce-scatter.4.cloned.1.call-update) | async-done | bytes 393232 | tf_op jit(solution)/shard_map/reduce_scatter | solution.py:90
  318.7 1.9 convert_element_type.65
  320.6 4.0 %copy.71 = bf16[2,8,96,1024]{3,2,1,0:T(8,128)(2,1)} copy(bf16[2,8,96,1024]{3,2,0,1:T(8,128)(2,1)} %all-to-all-done.1) | data formatting | bytes 6291456 | tf_op jit(solution)/shard_map/all_to_all | solution.py:71
  324.6 8.3 %gather_fusion = bf16[1024,1024]{1,0:T(8,128)(2,1)} fusion(bf16[1536,1024]{1,0:T(8,128)(2,1)} %bitcast.120, s32[1024]{0:T(1024)S(1)} %broadcast_clamp_fusion), kind=kCustom, calls=%fused_computation.1 | custom fusion | bytes 4198400 | tf_op jit(solution)/shard_map/gather | solution.py:60
  332.9 2.8 fusion.12
  335.7 0.7 copy.90
  336.4 3.7 multiply_reduce_fusion
  340.1 14.4 %all-to-all-done.3 = bf16[8,2,1,96,1024]{4,3,1,2,0:T(8,128)(2,1)} async-done(((bf16[8,2,1,96,1024]{4,3,1,2,0:T(8,128)(2,1)}), bf16[8,2,1,96,1024]{4,3,1,2,0:T(8,128)(2,1)}, u32[]{:S(2)}, u32[]{:S(2)}) %all-to-all-start.3) | async-done | bytes 3145760 | tf_op jit(solution)/shard_map/all_to_all | solution.py:78
  354.4 4.0 %copy.82 = bf16[2,8,1,96,1024]{4,3,1,0,2:T(8,128)(2,1)} copy(bf16[2,8,1,96,1024]{4,3,0,2,1:T(8,128)(2,1)} %bitcast.27) | data formatting | bytes 6291456 | tf_op jit(solution)/shard_map/reshape | solution.py:77
  358.4 8.4 %gather_fusion.1 = bf16[1024,1024]{1,0:T(8,128)(2,1)} fusion(bf16[1536,1024]{1,0:T(8,128)(2,1)} %bitcast.119, s32[1024]{0:T(1024)S(1)} %broadcast_clamp_fusion), kind=kCustom, calls=%fused_computation.2 | custom fusion | bytes 4198400 | tf_op jit(solution)/shard_map/gather | solution.py:60
  366.8 3.7 bitcast_reduce_fusion
  (28 shorter events, 0.2 us)
Async XLA Ops:
  7.2 179.9 %copy-start = (bf16[2,384,1024]{2,1,0:T(8,128)(2,1)S(1)}, bf16[2,384,1024]{2,1,0:T(8,128)(2,1)}, u32[]{:S(2)}) copy-start(bf16[2,384,1024]{2,1,0:T(8,128)(2,1)} %param.13) | copy-start | bytes 4718596
  34.2 7.4 %copy-start.9 = (f32[128,8]{0,1:T(8,128)S(1)}, f32[128,8]{0,1:T(8,128)}, u32[]{:S(2)}) copy-start(f32[128,8]{0,1:T(8,128)} %param.9) | copy-start | bytes 12292
  34.2 7.6 %copy-start.8 = (bf16[128,1024]{1,0:T(8,128)(2,1)S(1)}, bf16[128,1024]{1,0:T(8,128)(2,1)}, u32[]{:S(2)}) copy-start(bf16[128,1024]{1,0:T(8,128)(2,1)} %param.10) | copy-start | bytes 786436
  34.2 78.2 %all-to-all-start = ((bf16[2,8,96,1024]{3,2,0,1:T(8,128)(2,1)}), bf16[2,8,96,1024]{3,2,0,1:T(8,128)(2,1)}, u32[]{:S(2)}, u32[]{:S(2)}) async-start(bf16[2,8,96,1024]{3,2,0,1:T(8,128)(2,1)} %copy.67), calls=%async_computation | async-start | bytes 6291456 | tf_op jit(solution)/shard_map/all_to_all | solution.py:67
  53.6 63.5 %copy-start.2 = (bf16[2,1024,384]{2,1,0:T(8,128)(2,1)S(1)}, bf16[2,1024,384]{2,1,0:T(8,128)(2,1)}, u32[]{:S(2)}) copy-start(bf16[2,1024,384]{2,1,0:T(8,128)(2,1)} %param.12) | copy-start | bytes 4718596
  112.4 74.6 %all-to-all-start.2 = ((bf16[2,8,96,1024]{3,2,0,1:T(8,128)(2,1)}), bf16[2,8,96,1024]{3,2,0,1:T(8,128)(2,1)}, u32[]{:S(2)}, u32[]{:S(2)}) async-start(bf16[2,8,96,1024]{3,2,0,1:T(8,128)(2,1)} %copy.73), calls=%async_computation.2 | async-start | bytes 6291456 | tf_op jit(solution)/shard_map/all_to_all | solution.py:73
  116.9 172.6 %reduce-scatter.8.cloned.1.call-start = ((), (), s32[]{:S(2)}) async-start(), calls=%async_computation.9 | async-start | bytes 1966080 | tf_op jit(solution)/shard_map/reduce_scatter | solution.py:86
  117.2 5.3 %copy-start.3 = (bf16[2,1024,384]{2,1,0:T(8,128)(2,1)S(1)}, bf16[2,1024,384]{2,1,0:T(8,128)(2,1)}, u32[]{:S(2)}) copy-start(bf16[2,1024,384]{2,1,0:T(8,128)(2,1)} %param.11) | copy-start | bytes 4718596
  194.2 1.0 copy-start.10
  205.0 4.9 %copy-start.6 = (bf16[2,8,96,384]{3,2,1,0:T(8,128)(2,1)S(1)}, bf16[2,8,96,384]{3,2,1,0:T(8,128)(2,1)}, u32[]{:S(2)}) copy-start(bf16[2,8,96,384]{3,2,1,0:T(8,128)(2,1)} %get-tuple-element.6) | copy-start | bytes 3538948
  205.0 74.8 %all-to-all-start.1 = ((bf16[2,8,96,1024]{3,2,0,1:T(8,128)(2,1)}), bf16[2,8,96,1024]{3,2,0,1:T(8,128)(2,1)}, u32[]{:S(2)}, u32[]{:S(2)}) async-start(bf16[2,8,96,1024]{3,2,0,1:T(8,128)(2,1)} %copy.70), calls=%async_computation.1 | async-start | bytes 6291456 | tf_op jit(solution)/shard_map/all_to_all | solution.py:71
  209.6 81.9 %reduce-scatter.6.cloned.1.call-start = ((), (), s32[]{:S(2)}) async-start(), calls=%async_computation.8 | async-start | bytes 1966080 | tf_op jit(solution)/shard_map/reduce_scatter | solution.py:93
  214.8 1.6 copy-start.4
  216.4 3.2 copy-start.7
  227.7 56.9 %copy-start.5 = (bf16[2,8,96,384]{3,2,1,0:T(8,128)(2,1)S(1)}, bf16[2,8,96,384]{3,2,1,0:T(8,128)(2,1)}, u32[]{:S(2)}) copy-start(bf16[2,8,96,384]{3,2,1,0:T(8,128)(2,1)} %get-tuple-element.7) | copy-start | bytes 3538948
  279.8 74.6 %all-to-all-start.3 = ((bf16[8,2,1,96,1024]{4,3,1,2,0:T(8,128)(2,1)}), bf16[8,2,1,96,1024]{4,3,1,2,0:T(8,128)(2,1)}, u32[]{:S(2)}, u32[]{:S(2)}) async-start(bf16[8,2,1,96,1024]{4,3,1,2,0:T(8,128)(2,1)} %fusion.32), calls=%async_computation.3 | async-start | bytes 6291456 | tf_op jit(solution)/shard_map/all_to_all | solution.py:78
  284.2 34.5 %reduce-scatter.4.cloned.1.call-start = ((), (), s32[]{:S(2)}) async-start(), calls=%async_computation.7 | async-start | bytes 1966080 | tf_op jit(solution)/shard_map/reduce_scatter | solution.py:90
  358.4 12.2 %copy-start.1 = (bf16[2,384,1024]{2,1,0:T(8,128)(2,1)S(1)}, bf16[2,384,1024]{2,1,0:T(8,128)(2,1)}, u32[]{:S(2)}) copy-start(bf16[2,384,1024]{2,1,0:T(8,128)(2,1)} %param.13) | copy-start | bytes 4718596
Sparse Core Ops, SparseCore 0:
  199.9 27.0 reduce-scatter.7
  229.6 27.9 reduce-scatter.5
  289.6 29.0 reduce-scatter.3
